TPU v7x, 32 devices: a whole 2x2x4 slice. The times are simulated.
32 devices in a mesh: dp: 8 (over y, x, core), tensor: 4 (over z).
Axes of the slice: x: 2, y: 2, z: 4, core: 2. Of those that a mesh axis runs over, the one named last changes fastest.
Arguments:
- tokens: bfloat16 [4096, 1024], P(('dp', 'tensor')), may hold values from -6 to 6
- seg_ids: int32 [8, 512], P('dp'), may hold values from 0 to 3, never falling along the last dimension, each value on 1 to 256 neighbouring positions
- attn_gain: float32 [1024], replicated, may hold values from 0.5 to 1.5
- w_query: bfloat16 [1024, 1024], P(None, 'tensor'), may hold values from -0.1875 to 0.1875
- w_key: bfloat16 [1024, 1024], P(None, 'tensor'), may hold values from -0.1875 to 0.1875
- w_value: bfloat16 [1024, 2048], P(None, 'tensor'), may hold values from -0.1875 to 0.1875
- w_gate: bfloat16 [1024, 2048], P(None, 'tensor'), may hold values from -0.1875 to 0.1875
- w_decay: bfloat16 [1024, 8], P(None, 'tensor'), may hold values from -0.1875 to 0.1875
- w_beta: bfloat16 [1024, 8], P(None, 'tensor'), may hold values from -0.1875 to 0.1875
- conv_query: float32 [4, 1024], P(None, 'tensor'), may hold values from -3 to 3
- conv_key: float32 [4, 1024], P(None, 'tensor'), may hold values from -3 to 3
- conv_value: float32 [4, 2048], P(None, 'tensor'), may hold values from -3 to 3
- decay_rate: float32 [8], P('tensor'), may hold values from 0.005 to 1
- out_gain: float32 [256], replicated, may hold values from 0.5 to 1.5
- w_out: bfloat16 [2048, 1024], P('tensor'), may hold values from -0.25 to 0.25
- ffn_gain: float32 [1024], replicated, may hold values from 0.5 to 1.5
- w_ffn_gate: bfloat16 [1024, 2816], P(None, 'tensor'), may hold values from -0.1875 to 0.1875
- w_ffn_up: bfloat16 [1024, 2816], P(None, 'tensor'), may hold values from -0.1875 to 0.1875
- w_ffn_down: bfloat16 [2816, 1024], P('tensor'), may hold values from -0.21875 to 0.21875
- grad_out: bfloat16 [4096, 1024], P(('dp', 'tensor')), may hold values from -6 to 6
Outputs:
- block_out: bfloat16 [4096, 1024], P(('dp', 'tensor'))
- grad_tokens: bfloat16 [4096, 1024], P(('dp', 'tensor'))
- grad_attn_gain: float32 [1024], replicated
- grad_w_query: float32 [1024, 1024], P('dp', 'tensor')
- grad_w_key: float32 [1024, 1024], P('dp', 'tensor')
- grad_w_value: float32 [1024, 2048], P('dp', 'tensor')
- grad_w_gate: float32 [1024, 2048], P('dp', 'tensor')
- grad_w_decay: float32 [1024, 8], P('dp', 'tensor')
- grad_w_beta: float32 [1024, 8], P('dp', 'tensor')
- grad_conv_query: float32 [4, 1024], P(None, 'tensor')
- grad_conv_key: float32 [4, 1024], P(None, 'tensor')
- grad_conv_value: float32 [4, 2048], P(None, 'tensor')
- grad_decay_rate: float32 [8], P('tensor')
- grad_out_gain: float32 [256], replicated
- grad_w_out: float32 [2048, 1024], P('tensor', 'dp')
- grad_ffn_gain: float32 [1024], replicated
- grad_w_ffn_gate: float32 [1024, 2816], P('dp', 'tensor')
- grad_w_ffn_up: float32 [1024, 2816], P('dp', 'tensor')
- grad_w_ffn_down: float32 [2816, 1024], P('tensor', 'dp')
Inputs may be any that keep to these rules, and one draw needn't show every extreme that they name: `seg_ids`: along each sequence the document numbers never fall; each document has 1 to 256 tokens.
All inputs are finite; a program needn't handle non-finite values.
Results may differ from a plain program's by a relative error of at most 0.018.
Values may be sent and summed in bfloat16 or wider, within the bound.
A program may use at most 192 MiB of HBM per device.

v0:
```python
from functools import partial
import math

import jax
import jax.numpy as jnp
from jax import lax
from jax.sharding import PartitionSpec as P

GROUP = 64


EPS_NORM = 1e-05
EPS_UNIT = 1e-06
HIGH = lax.Precision.HIGHEST


def norm_gain(values, gain):
    return values * lax.rsqrt(jnp.mean(values * values, axis=-1, keepdims=True) + EPS_NORM) * gain


def shift_rows(values, offset, fill):
    padding = jnp.full((offset,) + values.shape[1:], fill, values.dtype)
    return jnp.concatenate([padding, values[:-offset]], axis=0)


def short_conv(values, taps, seg_row):
    total = taps[0] * values
    for offset in range(1, taps.shape[0]):
        keep = (seg_row == shift_rows(seg_row, offset, -1)).astype(values.dtype)
        total = total + taps[offset] * shift_rows(values, offset, 0) * keep[:, None]
    return total


def unit_rows(values):
    return values * lax.rsqrt(jnp.sum(values * values, axis=-1, keepdims=True) + EPS_UNIT)


def delta_block(carry, block):
    state, prev_doc = carry
    query, keys, values, beta, log_decay, doc = block
    size = doc.shape[0]
    index = jnp.arange(size)
    lower = index[:, None] >= index[None, :]
    strict = (index[:, None] > index[None, :]).astype(state.dtype)
    same_doc = ((doc[:, None] == doc[None, :]) & lower).astype(state.dtype)
    cum_log = jnp.cumsum(log_decay, axis=0).T
    spread = jnp.exp(jnp.minimum(cum_log[:, :, None] - cum_log[:, None, :], 0.0)) * same_doc[None]
    carried_keep = jnp.exp(cum_log) * (doc == prev_doc).astype(state.dtype)[None, :]
    key_key = jnp.einsum("thd,ihd->hti", keys, keys, precision=HIGH)
    beta_rows = beta.T[:, :, None]
    system = jnp.eye(size, dtype=state.dtype)[None] + beta_rows * key_key * spread * strict[None]
    from_state = jnp.einsum("thd,hde->hte", keys, state, precision=HIGH)
    right_side = beta_rows * (
        jnp.transpose(values, (1, 0, 2)) - carried_keep[:, :, None] * from_state
    )
    delta = lax.linalg.triangular_solve(
        system, right_side, left_side=True, lower=True, unit_diagonal=True
    )
    query_key = jnp.einsum("thd,ihd->hti", query, keys, precision=HIGH)
    mixed = jnp.einsum("hti,hie->the", query_key * spread, delta, precision=HIGH)
    mixed = mixed + jnp.einsum(
        "thd,hde->the", query * carried_keep.T[:, :, None], state, precision=HIGH
    )
    final_row = spread[:, -1, :]
    new_state = carried_keep[:, -1][:, None, None] * state + jnp.einsum(
        "ihd,hi,hie->hde", keys, final_row, delta, precision=HIGH
    )
    return ((new_state, doc[-1]), mixed)


def mixer(
    seg_row,
    q_proj,
    k_proj,
    v_proj,
    gate_proj,
    decay_proj,
    beta_proj,
    conv_query,
    conv_key,
    conv_value,
    decay_rate,
    out_gain,
):
    length = q_proj.shape[0]
    heads = decay_proj.shape[1]
    key_dim = q_proj.shape[1] // heads
    val_dim = v_proj.shape[1] // heads
    query = unit_rows(
        jax.nn.silu(short_conv(q_proj, conv_query, seg_row)).reshape(length, heads, key_dim)
    ) / math.sqrt(key_dim)
    keys = unit_rows(
        jax.nn.silu(short_conv(k_proj, conv_key, seg_row)).reshape(length, heads, key_dim)
    )
    values = jax.nn.silu(short_conv(v_proj, conv_value, seg_row)).reshape(length, heads, val_dim)
    beta = jax.nn.sigmoid(beta_proj)
    log_decay = -decay_rate[None, :] * jax.nn.softplus(decay_proj)
    blocks = length // GROUP

    def split(array):
        return array.reshape((blocks, GROUP) + array.shape[1:])

    init = (jnp.zeros((heads, key_dim, val_dim), q_proj.dtype), jnp.array(-1, dtype=seg_row.dtype))
    _, mixed = lax.scan(
        delta_block,
        init,
        (split(query), split(keys), split(values), split(beta), split(log_decay), split(seg_row)),
    )
    mixed = mixed.reshape(length, heads, val_dim)
    gate = gate_proj.reshape(length, heads, val_dim)
    normed = (
        mixed
        * lax.rsqrt(jnp.mean(mixed * mixed, axis=-1, keepdims=True) + EPS_NORM)
        * out_gain
        * jax.nn.silu(gate)
    )
    return normed.reshape(length, heads * val_dim)


def body(
    tokens,
    seg_ids,
    attn_gain,
    w_query,
    w_key,
    w_value,
    w_gate,
    w_decay,
    w_beta,
    conv_query,
    conv_key,
    conv_value,
    decay_rate,
    out_gain,
    w_out,
    ffn_gain,
    w_ffn_gate,
    w_ffn_up,
    w_ffn_down,
    grad_out,
):
    seg_row = seg_ids[0]
    row_count = tokens.shape[0]
    mats = (w_query, w_key, w_value, w_gate, w_decay, w_beta)
    x_float = tokens.astype(jnp.float32)
    xnorm_rows = norm_gain(x_float, attn_gain).astype(jnp.bfloat16)
    xnorm = lax.all_gather(xnorm_rows, "tensor", axis=0, tiled=True)
    projs = [jnp.dot(xnorm, weight, preferred_element_type=jnp.float32) for weight in mats]
    mixed, pull_mix = jax.vjp(
        partial(mixer, seg_row),
        projs[0],
        projs[1],
        projs[2],
        projs[3],
        projs[4],
        projs[5],
        conv_query,
        conv_key,
        conv_value,
        decay_rate,
        out_gain,
    )
    gated = mixed.astype(jnp.bfloat16)
    rows_part = gated
    resid = x_float + lax.psum_scatter(
        jnp.dot(rows_part, w_out, preferred_element_type=jnp.float32),
        "tensor",
        scatter_dimension=0,
        tiled=True,
    )
    hnorm_rows = norm_gain(resid, ffn_gain).astype(jnp.bfloat16)
    hnorm = lax.all_gather(hnorm_rows, "tensor", axis=0, tiled=True)
    up_in = jnp.dot(hnorm, w_ffn_gate, preferred_element_type=jnp.float32)
    up_val = jnp.dot(hnorm, w_ffn_up, preferred_element_type=jnp.float32)
    act = (jax.nn.silu(up_in) * up_val).astype(jnp.bfloat16)
    rows_part = act
    block_out = (
        resid
        + lax.psum_scatter(
            jnp.dot(rows_part, w_ffn_down, preferred_element_type=jnp.float32).astype(jnp.bfloat16),
            "tensor",
            scatter_dimension=0,
            tiled=True,
        ).astype(jnp.float32)
    ).astype(jnp.bfloat16)
    grad_full = lax.all_gather(grad_out, "tensor", axis=0, tiled=True)
    d_act = jnp.einsum("td,fd->tf", grad_full, w_ffn_down, preferred_element_type=jnp.float32)
    g_down = jnp.einsum("tf,td->fd", act, grad_full, preferred_element_type=jnp.float32)
    gate_sig = jax.nn.sigmoid(up_in)
    d_up_in = (d_act * up_val * gate_sig * (1.0 + up_in * (1.0 - gate_sig))).astype(jnp.bfloat16)
    d_up_val = (d_act * up_in * gate_sig).astype(jnp.bfloat16)
    g_fgate = jnp.einsum("td,tf->df", hnorm, d_up_in, preferred_element_type=jnp.float32)
    g_fup = jnp.einsum("td,tf->df", hnorm, d_up_val, preferred_element_type=jnp.float32)
    total = jnp.einsum("tf,df->td", d_up_in, w_ffn_gate, preferred_element_type=jnp.float32)
    d_hnorm = lax.psum_scatter(
        (
            total + jnp.einsum("tf,df->td", d_up_val, w_ffn_up, preferred_element_type=jnp.float32)
        ).astype(jnp.bfloat16),
        "tensor",
        scatter_dimension=0,
        tiled=True,
    ).astype(jnp.float32)
    _, pull_mid = jax.vjp(norm_gain, resid, ffn_gain)
    d_resid_norm, g_fgain = pull_mid(d_hnorm)
    d_resid = grad_out.astype(jnp.float32) + d_resid_norm
    d_resid_full = lax.all_gather(d_resid.astype(jnp.bfloat16), "tensor", axis=0, tiled=True)
    g_out = jnp.einsum("tc,td->cd", gated, d_resid_full, preferred_element_type=jnp.float32)
    d_gated = jnp.einsum("td,cd->tc", d_resid_full, w_out, preferred_element_type=jnp.float32)
    back = pull_mix(d_gated)
    d_projs = [grad.astype(jnp.bfloat16) for grad in back[:6]]
    g_mats = [
        jnp.einsum("td,tc->dc", xnorm, grad, preferred_element_type=jnp.float32) for grad in d_projs
    ]
    total = jnp.zeros((row_count * lax.axis_size("tensor"), xnorm.shape[1]), jnp.float32)
    for grad, weight in zip(d_projs, mats):
        total = total + jnp.einsum("tc,dc->td", grad, weight, preferred_element_type=jnp.float32)
    d_xnorm = lax.psum_scatter(
        total.astype(jnp.bfloat16), "tensor", scatter_dimension=0, tiled=True
    ).astype(jnp.float32)
    _, pull_first = jax.vjp(norm_gain, x_float, attn_gain)
    d_x_norm, g_again = pull_first(d_xnorm)
    grad_tokens = (d_resid + d_x_norm).astype(jnp.bfloat16)
    weight_sums = (
        lax.psum_scatter(g_mats[0], "dp", scatter_dimension=0, tiled=True),
        lax.psum_scatter(g_mats[1], "dp", scatter_dimension=0, tiled=True),
        lax.psum_scatter(g_mats[2], "dp", scatter_dimension=0, tiled=True),
        lax.psum_scatter(g_mats[3], "dp", scatter_dimension=0, tiled=True),
        lax.psum_scatter(g_mats[4], "dp", scatter_dimension=0, tiled=True),
        lax.psum_scatter(g_mats[5], "dp", scatter_dimension=0, tiled=True),
        lax.psum_scatter(g_out, "dp", scatter_dimension=1, tiled=True),
        lax.psum_scatter(g_fgate, "dp", scatter_dimension=0, tiled=True),
        lax.psum_scatter(g_fup, "dp", scatter_dimension=0, tiled=True),
        lax.psum_scatter(g_down, "dp", scatter_dimension=1, tiled=True),
    )
    rate_parts = lax.psum((back[6], back[7], back[8], back[9]), "dp")
    gain_parts = lax.psum((g_again, g_fgain, back[10]), ("dp", "tensor"))
    return (
        block_out,
        grad_tokens,
        gain_parts[0],
        weight_sums[0],
        weight_sums[1],
        weight_sums[2],
        weight_sums[3],
        weight_sums[4],
        weight_sums[5],
        rate_parts[0],
        rate_parts[1],
        rate_parts[2],
        rate_parts[3],
        gain_parts[2],
        weight_sums[6],
        gain_parts[1],
        weight_sums[7],
        weight_sums[8],
        weight_sums[9],
    )


def solution(mesh):
    in_specs = (
        P(("dp", "tensor"), None),
        P("dp", None),
        P(),
        P(None, "tensor"),
        P(None, "tensor"),
        P(None, "tensor"),
        P(None, "tensor"),
        P(None, "tensor"),
        P(None, "tensor"),
        P(None, "tensor"),
        P(None, "tensor"),
        P(None, "tensor"),
        P("tensor"),
        P(),
        P("tensor", None),
        P(),
        P(None, "tensor"),
        P(None, "tensor"),
        P("tensor", None),
        P(("dp", "tensor"), None),
    )
    out_specs = (
        P(("dp", "tensor"), None),
        P(("dp", "tensor"), None),
        P(),
        P("dp", "tensor"),
        P("dp", "tensor"),
        P("dp", "tensor"),
        P("dp", "tensor"),
        P("dp", "tensor"),
        P("dp", "tensor"),
        P(None, "tensor"),
        P(None, "tensor"),
        P(None, "tensor"),
        P("tensor"),
        P(),
        P("tensor", "dp"),
        P(),
        P("dp", "tensor"),
        P("dp", "tensor"),
        P("tensor", "dp"),
    )
    return jax.shard_map(body, mesh=mesh, in_specs=in_specs, out_specs=out_specs, check_vma=False)
```

profile of v0, /device:TPU:0, one launch (start us, length us, event | category | flops | bytes accessed | tf_op | source)
XLA Modules:
  0.0 1341.3 jit_solution(10986479846402996442)
XLA Ops:
  19.1 23.2 %all-gather.5.cloned.1.call-done = bf16[512,1024]{1,0:T(8,128)(2,1)} async-done(((bf16[128,1024]{1,0:T(8,128)(2,1)}), bf16[512,1024]{1,0:T(8,128)(2,1)}) %all-gather.5.cloned.1.call-update) | async-done | bytes 1048592 | tf_op jit(solution)/shard_map/all_gather | solution.py:147
  49.5 2.3 copy.242
  54.0 2.1 reshape.599
  59.6 2.1 fusion.180
  61.8 2.9 reshape.602
  68.1 221.8 %while.86 = (s32[]{:T(128)}, f32[2,128,256]{2,1,0:T(8,128)S(1)}, s32[]{:T(128)}, f32[8,64,2,256]{3,1,2,0:T(8,128)}, f32[8,2,64,64]{3,2,1,0:T(8,128)}, /*index=5*...) while((s32[]{:T(128)}, f32[2,128,256]{2,1,0:T(8,128)S(1)}, ...), condition=%wide.region_5.6_spmd.clone.clone, body=%wide.region_3.5_spmd.clone.clone.sunk | while | flops 227480128 | bytes 5427070 | solution.py:104
  73.7 9.8 custom-call.44
  101.3 9.8 custom-call.44
  129.0 9.8 custom-call.44
  156.7 9.8 custom-call.44
  184.4 9.8 custom-call.44
  212.1 9.8 custom-call.44
  239.7 9.8 custom-call.44
  267.4 9.8 custom-call.44
  300.0 2.1 fusion.235
  302.1 43.1 %reduce-scatter.19.cloned.1.call-done = f32[128,1024]{1,0:T(8,128)} async-done(((f32[512,1024]{1,0:T(8,128)}), f32[128,1024]{1,0:T(8,128)}) %reduce-scatter.19.cloned.1.call-update) | async-done | bytes 524304 | tf_op jit(solution)/shard_map/reduce_scatter | solution.py:165
  348.0 26.7 %all-gather.7.cloned.1.call-done = bf16[512,1024]{1,0:T(8,128)(2,1)} async-done(((bf16[128,1024]{1,0:T(8,128)(2,1)}), bf16[512,1024]{1,0:T(8,128)(2,1)}) %all-gather.7.cloned.1.call-update) | async-done | bytes 1048592 | tf_op jit(solution)/shard_map/all_gather | solution.py:172
  374.7 4.0 fusion.236
  378.6 2.1 fusion.237
  380.8 22.7 %all-gather.9.cloned.1.call-done = bf16[512,1024]{1,0:T(8,128)(2,1)} async-done(((bf16[128,1024]{1,0:T(8,128)(2,1)}), bf16[512,1024]{1,0:T(8,128)(2,1)}) %all-gather.9.cloned.1.call-update) | async-done | bytes 1048592 | tf_op jit(solution)/shard_map/all_gather | solution.py:186
  403.5 4.6 multiply_convert_fusion
  412.0 26.8 %reduce-scatter.23.cloned.1.call-done = bf16[128,1024]{1,0:T(8,128)(2,1)} async-done(((bf16[512,1024]{1,0:T(8,128)(2,1)}), bf16[128,1024]{1,0:T(8,128)(2,1)}) %reduce-scatter.23.cloned.1.call-update) | async-done | bytes 262160 | tf_op jit(solution)/shard_map/reduce_scatter | solution.py:195
  444.7 2.9 reshape.607
  450.6 19.7 %all-gather.11.cloned.1.call-done = bf16[512,1024]{1,0:T(8,128)(2,1)} async-done(((bf16[128,1024]{1,0:T(8,128)(2,1)}), bf16[512,1024]{1,0:T(8,128)(2,1)}) %all-gather.11.cloned.1.call-update) | async-done | bytes 1048592 | tf_op jit(solution)/shard_map/all_gather | solution.py:206
  470.3 4.6 fusion.179
  474.9 2.9 reshape.606
  477.7 3.1 multiply_reduce_fusion
  485.2 309.4 %while.85 = (s32[]{:T(128)}, f32[2,128,256]{2,1,0:T(8,128)S(1)}, f32[8,64,2,128]{3,1,2,0:T(8,128)}, f32[8,64,2,128]{3,1,2,0:T(8,128)}, f32[8,64,2,256]{3,2,1,0:T...) while((s32[]{:T(128)}, f32[2,128,256]{2,1,0:T(8,128)S(1)}, ...), condition=%wide.region_22.23_spmd.clone, body=%wide.region_13.22_spmd.clone.sunk | while | flops 460771392 | bytes 8059096 | solution.py:104
  491.9 9.8 custom-call.43
  530.6 9.8 custom-call.43
  569.2 9.8 custom-call.43
  607.9 9.8 custom-call.43
  646.5 9.8 custom-call.43
  685.2 9.8 custom-call.43
  723.8 9.8 custom-call.43
  762.5 9.8 custom-call.43
  794.7 2.1 broadcast_multiply_fusion.4
  796.8 2.4 copy.284
  800.0 2.5 copy.285
  811.4 2.3 reshape.636
  813.7 2.4 reshape.637
  816.1 3.3 multiply_reduce_fusion.10
  837.7 2.2 fusion.241
  840.0 3.3 fusion.242
  847.9 5.8 add_convert_fusion
  854.0 3.3 convolution_convert_fusion
  857.4 3.6 fusion.249
  861.1 3.7 fusion.250
  865.8 3.7 fusion.248
  873.6 3.3 fusion.247
  879.3 2.1 fusion.246
  881.8 24.2 %all-reduce.35 = (f32[4,256]{1,0:T(4,128)}, f32[4,256]{1,0:T(4,128)}, f32[4,512]{1,0:T(4,128)}, f32[2]{0:T(128)}) all-reduce(f32[4,256]{1,0:T(4,128)S(1)} %pad_add_fusion.2, f32[4,256]{1,0:T(4,128)S(1)} %pad_add_fusion.1, f32[4,512]{1,0:T(4,128)S(1)} %pad_add_fusion, f32[2]{0:T(128)S(1)} %neg.74), channel_id=1, replica_groups=mesh['dp'=8,'tensor'=4] {'dp'}, use_global_device_ids=true, to_apply=%region_39.40 | all-reduce | flops 4098 | bytes 32784 | tf_op jit(solution)/shard_map/psum | solution.py:235
  907.4 10.0 reduce-scatter.45.cloned.1.call-done
  918.9 28.1 %reduce-scatter.25.cloned.1.call-done = bf16[128,1024]{1,0:T(8,128)(2,1)} async-done(((bf16[512,1024]{1,0:T(8,128)(2,1)}), bf16[128,1024]{1,0:T(8,128)(2,1)}) %reduce-scatter.25.cloned.1.call-update) | async-done | bytes 262160 | tf_op jit(solution)/shard_map/reduce_scatter | solution.py:217
  948.2 40.0 %all-reduce.34 = (f32[1024]{0:T(1024)}, f32[256]{0:T(256)}, f32[1024]{0:T(1024)}) all-reduce(f32[1024]{0:T(1024)S(1)} %get-tuple-element.1526, f32[256]{0:T(256)S(1)} %copy-done.130, f32[1024]{0:T(1024)S(1)} %copy-done.96), channel_id=1, replica_groups=mesh['dp'=8,'tensor'=4] {'dp','tensor'}, use_global_device_ids=true, to_apply=%region_28.29 | all-reduce | flops 2304 | bytes 18432 | tf_op jit(solution)/shard_map/psum | solution.py:236
  988.3 2.1 fusion.195
  990.4 32.6 %reduce-scatter.37.cloned.1.call-done = f32[128,704]{0,1:T(8,128)} async-done(((f32[1024,704]{0,1:T(8,128)}), f32[128,704]{0,1:T(8,128)}) %reduce-scatter.37.cloned.1.call-update) | async-done | bytes 360464 | tf_op jit(solution)/shard_map/reduce_scatter | solution.py:231
  1023.0 48.6 %reduce-scatter.39.cloned.1.call-done = f32[128,704]{0,1:T(8,128)} async-done(((f32[1024,704]{0,1:T(8,128)}), f32[128,704]{0,1:T(8,128)}) %reduce-scatter.39.cloned.1.call-update) | async-done | bytes 360464 | tf_op jit(solution)/shard_map/reduce_scatter | solution.py:232
  1071.6 48.7 %reduce-scatter.41.cloned.1.call-done = f32[704,128]{1,0:T(8,128)} async-done(((f32[704,1024]{1,0:T(8,128)}), f32[704,128]{1,0:T(8,128)}) %reduce-scatter.41.cloned.1.call-update) | async-done | bytes 360464 | tf_op jit(solution)/shard_map/reduce_scatter | solution.py:233
  1120.3 39.6 %reduce-scatter.29.cloned.1.call-done = f32[128,256]{1,0:T(8,128)} async-done(((f32[1024,256]{1,0:T(8,128)}), f32[128,256]{1,0:T(8,128)}) %reduce-scatter.29.cloned.1.call-update) | async-done | bytes 131088 | tf_op jit(solution)/shard_map/reduce_scatter | solution.py:225
  1159.9 39.6 %reduce-scatter.27.cloned.1.call-done = f32[128,256]{1,0:T(8,128)} async-done(((f32[1024,256]{1,0:T(8,128)}), f32[128,256]{1,0:T(8,128)}) %reduce-scatter.27.cloned.1.call-update) | async-done | bytes 131088 | tf_op jit(solution)/shard_map/reduce_scatter | solution.py:224
  1199.5 44.9 %reduce-scatter.35.cloned.1.call-done = f32[512,128]{1,0:T(8,128)} async-done(((f32[512,1024]{1,0:T(8,128)}), f32[512,128]{1,0:T(8,128)}) %reduce-scatter.35.cloned.1.call-update) | async-done | bytes 262160 | tf_op jit(solution)/shard_map/reduce_scatter | solution.py:230
  1244.3 44.9 %reduce-scatter.31.cloned.1.call-done = f32[128,512]{1,0:T(8,128)} async-done(((f32[1024,512]{1,0:T(8,128)}), f32[128,512]{1,0:T(8,128)}) %reduce-scatter.31.cloned.1.call-update) | async-done | bytes 262160 | tf_op jit(solution)/shard_map/reduce_scatter | solution.py:226
  1289.2 44.9 %reduce-scatter.33.cloned.1.call-done = f32[128,512]{1,0:T(8,128)} async-done(((f32[1024,512]{1,0:T(8,128)}), f32[128,512]{1,0:T(8,128)}) %reduce-scatter.33.cloned.1.call-update) | async-done | bytes 262160 | tf_op jit(solution)/shard_map/reduce_scatter | solution.py:227
  (1018 shorter events, 468.5 us)
Async XLA Ops:
  7.2 396.3 %copy-start = (bf16[704,1024]{1,0:T(8,128)(2,1)S(1)}, bf16[704,1024]{1,0:T(8,128)(2,1)}, u32[]{:S(2)}) copy-start(bf16[704,1024]{1,0:T(8,128)(2,1)} %param.42) | copy-start | bytes 4325380
  7.2 37.0 %copy-start.53 = (bf16[1024,256]{1,0:T(8,128)(2,1)S(1)}, bf16[1024,256]{1,0:T(8,128)(2,1)}, u32[]{:S(2)}) copy-start(bf16[1024,256]{1,0:T(8,128)(2,1)} %param.28) | copy-start | bytes 1572868
  7.2 35.0 %all-gather.5.cloned.1.call-start = ((), (), s32[]{:S(2)}) async-start(), calls=%async_computation.14 | async-start | bytes 1310720 | tf_op jit(solution)/shard_map/all_gather | solution.py:147
  11.4 333.9 %reduce-scatter.19.cloned.1.call-start = ((), (), s32[]{:S(2)}) async-start(), calls=%async_computation.15 | async-start | bytes 2621440 | tf_op jit(solution)/shard_map/reduce_scatter | solution.py:165
  12.3 52.4 %copy-start.119 = (f32[2]{0:T(128)}, f32[2]{0:T(128)S(1)}, u32[]{:S(2)}) copy-start(f32[2]{0:T(128)S(1)} %neg.65) | copy-start | bytes 28
  16.3 28.4 %copy-start.99 = (f32[1,256]{1,0:T(1,128)}, f32[1,256]{1,0:T(1,128)S(1)}, u32[]{:S(2)}) copy-start(f32[1,256]{1,0:T(1,128)S(1)} %get-tuple-element.1770) | copy-start | bytes 3076
  16.3 28.4 %copy-start.106 = (f32[1,256]{1,0:T(1,128)}, f32[1,256]{1,0:T(1,128)S(1)}, u32[]{:S(2)}) copy-start(f32[1,256]{1,0:T(1,128)S(1)} %get-tuple-element.1772) | copy-start | bytes 3076
  16.3 28.4 %copy-start.110 = (f32[1,256]{1,0:T(1,128)}, f32[1,256]{1,0:T(1,128)S(1)}, u32[]{:S(2)}) copy-start(f32[1,256]{1,0:T(1,128)S(1)} %get-tuple-element.1773) | copy-start | bytes 3076
  16.4 28.4 %copy-start.112 = (f32[1,256]{1,0:T(1,128)}, f32[1,256]{1,0:T(1,128)S(1)}, u32[]{:S(2)}) copy-start(f32[1,256]{1,0:T(1,128)S(1)} %get-tuple-element.1771) | copy-start | bytes 3076
  17.2 27.5 %copy-start.97 = (f32[1,256]{1,0:T(1,128)}, f32[1,256]{1,0:T(1,128)S(1)}, u32[]{:S(2)}) copy-start(f32[1,256]{1,0:T(1,128)S(1)} %get-tuple-element.1766) | copy-start | bytes 3076
  17.2 27.5 %copy-start.102 = (f32[1,256]{1,0:T(1,128)}, f32[1,256]{1,0:T(1,128)S(1)}, u32[]{:S(2)}) copy-start(f32[1,256]{1,0:T(1,128)S(1)} %get-tuple-element.1768) | copy-start | bytes 3076
  17.2 27.6 %copy-start.104 = (f32[1,256]{1,0:T(1,128)}, f32[1,256]{1,0:T(1,128)S(1)}, u32[]{:S(2)}) copy-start(f32[1,256]{1,0:T(1,128)S(1)} %get-tuple-element.1767) | copy-start | bytes 3076
  17.2 27.6 %copy-start.108 = (f32[1,256]{1,0:T(1,128)}, f32[1,256]{1,0:T(1,128)S(1)}, u32[]{:S(2)}) copy-start(f32[1,256]{1,0:T(1,128)S(1)} %get-tuple-element.1769) | copy-start | bytes 3076
  18.1 41.4 %copy-start.69 = (f32[512]{0:T(512)}, f32[512]{0:T(512)S(1)}, u32[]{:S(2)}) copy-start(f32[512]{0:T(512)S(1)} %get-tuple-element.1777) | copy-start | bytes 6148
  18.1 41.4 %copy-start.71 = (f32[512]{0:T(512)}, f32[512]{0:T(512)S(1)}, u32[]{:S(2)}) copy-start(f32[512]{0:T(512)S(1)} %get-tuple-element.1779) | copy-start | bytes 6148
  18.2 41.4 %copy-start.73 = (f32[512]{0:T(512)}, f32[512]{0:T(512)S(1)}, u32[]{:S(2)}) copy-start(f32[512]{0:T(512)S(1)} %get-tuple-element.1778) | copy-start | bytes 6148
  19.0 40.6 %copy-start.84 = (f32[1,512]{1,0:T(1,128)}, f32[1,512]{1,0:T(1,128)S(1)}, u32[]{:S(2)}) copy-start(f32[1,512]{1,0:T(1,128)S(1)} %get-tuple-element.1754) | copy-start | bytes 6148
  19.0 40.6 %copy-start.86 = (f32[1,512]{1,0:T(1,128)}, f32[1,512]{1,0:T(1,128)S(1)}, u32[]{:S(2)}) copy-start(f32[1,512]{1,0:T(1,128)S(1)} %get-tuple-element.1756) | copy-start | bytes 6148
  19.0 40.6 %copy-start.88 = (f32[1,512]{1,0:T(1,128)}, f32[1,512]{1,0:T(1,128)S(1)}, u32[]{:S(2)}) copy-start(f32[1,512]{1,0:T(1,128)S(1)} %get-tuple-element.1755) | copy-start | bytes 6148
  19.1 40.6 %copy-start.90 = (f32[1,512]{1,0:T(1,128)}, f32[1,512]{1,0:T(1,128)S(1)}, u32[]{:S(2)}) copy-start(f32[1,512]{1,0:T(1,128)S(1)} %get-tuple-element.1757) | copy-start | bytes 6148
  46.4 5.5 copy-start.78
  46.4 5.4 copy-start.80
  48.2 5.7 copy-start.22
  51.8 7.0 copy-start.76
  61.8 4.5 copy-start.48
  300.0 45.3 %copy-start.14 = (bf16[128,1024]{1,0:T(8,128)(2,1)S(1)}, bf16[128,1024]{1,0:T(8,128)(2,1)}, u32[]{:S(2)}) copy-start(bf16[128,1024]{1,0:T(8,128)(2,1)} %param.24) | copy-start | bytes 786436
  302.0 44.4 %copy-start.64 = (f32[1024]{0:T(1024)S(1)}, f32[1024]{0:T(1024)}, u32[]{:S(2)}) copy-start(f32[1024]{0:T(1024)} %param.39) | copy-start | bytes 12292
  302.1 72.6 %all-gather.7.cloned.1.call-start = ((), (), s32[]{:S(2)}) async-start(), calls=%async_computation.16 | async-start | bytes 1310720 | tf_op jit(solution)/shard_map/all_gather | solution.py:172
  346.4 32.2 %copy-start.138 = (f32[128]{0:T(128)}, f32[128]{0:T(128)S(1)}, u32[]{:S(2)}) copy-start(f32[128]{0:T(128)S(1)} %get-tuple-element.1691) | copy-start | bytes 1540
  346.4 94.8 %copy-start.10 = (f32[128,1024]{1,0:T(8,128)}, f32[128,1024]{1,0:T(8,128)S(1)}, u32[]{:S(2)}) copy-start(f32[128,1024]{1,0:T(8,128)S(1)} %get-tuple-element.1692) | copy-start | bytes 1572868
  346.5 94.7 %copy-start.117 = (f32[128]{0:T(128)}, f32[128]{0:T(128)S(1)}, u32[]{:S(2)}) copy-start(f32[128]{0:T(128)S(1)} %fusion.215) | copy-start | bytes 1540
  347.3 56.1 %all-gather.9.cloned.1.call-start = ((), (), s32[]{:S(2)}) async-start(), calls=%async_computation.18 | async-start | bytes 1310720 | tf_op jit(solution)/shard_map/all_gather | solution.py:186
  347.9 90.9 %reduce-scatter.23.cloned.1.call-start = ((), (), s32[]{:S(2)}) async-start(), calls=%async_computation.19 | async-start | bytes 1310720 | tf_op jit(solution)/shard_map/reduce_scatter | solution.py:195
  403.5 4.6 copy-start.139
  412.0 35.5 %copy-start.23 = (f32[512,256]{0,1:T(8,128)S(1)}, f32[512,256]{0,1:T(8,128)}, u32[]{:S(2)}) copy-start(f32[512,256]{0,1:T(8,128)} %copy-done.22) | copy-start | bytes 1572868
  412.0 58.3 %all-gather.11.cloned.1.call-start = ((), (), s32[]{:S(2)}) async-start(), calls=%async_computation.20 | async-start | bytes 1310720 | tf_op jit(solution)/shard_map/all_gather | solution.py:206
  443.6 462.3 %reduce-scatter.43.cloned.1.call-start = ((), (), s32[]{:S(2)}) async-start(), calls=%async_computation.30 | async-start | bytes 589824
  444.7 25.6 %copy-start.133 = (f32[1,2,2,128]{3,1,2,0:T(2,128)S(1)}, f32[1,2,2,128]{3,1,2,0:T(2,128)}, u32[]{:S(2)}) copy-start(f32[1,2,2,128]{3,1,2,0:T(2,128)} %copy.359) | copy-start | bytes 6148
  794.7 4.5 copy-start.62
  810.6 5.5 copy-start.77
  823.2 5.3 copy-start.100
  846.5 70.9 %reduce-scatter.45.cloned.1.call-start = ((), (), s32[]{:S(2)}) async-start(), calls=%async_computation.31 | async-start | bytes 589824
  847.9 99.2 %reduce-scatter.25.cloned.1.call-start = ((), (), s32[]{:S(2)}) async-start(), calls=%async_computation.21 | async-start | bytes 1310720 | tf_op jit(solution)/shard_map/reduce_scatter | solution.py:217
  853.7 134.5 %reduce-scatter.21.cloned.1.call-start = ((), (), s32[]{:S(2)}) async-start(), calls=%async_computation.17 | async-start | bytes 1310720 | tf_op jit(solution)/shard_map/reduce_scatter | solution.py:179
  857.3 165.7 %reduce-scatter.37.cloned.1.call-start = ((), (), s32[]{:S(2)}) async-start(), calls=%async_computation.27 | async-start | bytes 3244032 | tf_op jit(solution)/shard_map/reduce_scatter | solution.py:231
  861.0 210.6 %reduce-scatter.39.cloned.1.call-start = ((), (), s32[]{:S(2)}) async-start(), calls=%async_computation.28 | async-start | bytes 3244032 | tf_op jit(solution)/shard_map/reduce_scatter | solution.py:232
  864.7 255.5 %reduce-scatter.41.cloned.1.call-start = ((), (), s32[]{:S(2)}) async-start(), calls=%async_computation.29 | async-start | bytes 3244032 | tf_op jit(solution)/shard_map/reduce_scatter | solution.py:233
  869.6 290.3 %reduce-scatter.29.cloned.1.call-start = ((), (), s32[]{:S(2)}) async-start(), calls=%async_computation.23 | async-start | bytes 1179648 | tf_op jit(solution)/shard_map/reduce_scatter | solution.py:225
  872.0 327.5 %reduce-scatter.27.cloned.1.call-start = ((), (), s32[]{:S(2)}) async-start(), calls=%async_computation.22 | async-start | bytes 1179648 | tf_op jit(solution)/shard_map/reduce_scatter | solution.py:224
  873.6 370.8 %reduce-scatter.35.cloned.1.call-start = ((), (), s32[]{:S(2)}) async-start(), calls=%async_computation.26 | async-start | bytes 2359296 | tf_op jit(solution)/shard_map/reduce_scatter | solution.py:230
  877.0 412.2 %reduce-scatter.31.cloned.1.call-start = ((), (), s32[]{:S(2)}) async-start(), calls=%async_computation.24 | async-start | bytes 2359296 | tf_op jit(solution)/shard_map/reduce_scatter | solution.py:226
  879.2 67.8 %copy-start.15 = (bf16[128,1024]{1,0:T(8,128)(2,1)S(1)}, bf16[128,1024]{1,0:T(8,128)(2,1)}, u32[]{:S(2)}) copy-start(bf16[128,1024]{1,0:T(8,128)(2,1)} %param.24) | copy-start | bytes 786436
  879.2 67.8 %copy-start.75 = (f32[1024]{0:T(1024)S(1)}, f32[1024]{0:T(1024)}, u32[]{:S(2)}) copy-start(f32[1024]{0:T(1024)} %param.26) | copy-start | bytes 12292
  879.2 67.8 %copy-start.122 = (f32[128]{0:T(128)S(1)}, f32[128]{0:T(128)}, u32[]{:S(2)}) copy-start(f32[128]{0:T(128)} %copy-done.121) | copy-start | bytes 1540
  879.2 454.8 %reduce-scatter.33.cloned.1.call-start = ((), (), s32[]{:S(2)}) async-start(), calls=%async_computation.25 | async-start | bytes 2359296 | tf_op jit(solution)/shard_map/reduce_scatter | solution.py:227
  881.4 66.8 %copy-start.96 = (f32[1024]{0:T(1024)S(1)}, f32[1024]{0:T(1024)}, u32[]{:S(2)}) copy-start(f32[1024]{0:T(1024)} %get-tuple-element.1524) | copy-start | bytes 12292
  881.4 66.8 %copy-start.130 = (f32[256]{0:T(256)S(1)}, f32[256]{0:T(256)}, u32[]{:S(2)}) copy-start(f32[256]{0:T(256)} %get-tuple-element.1522) | copy-start | bytes 3076
  881.4 106.8 %copy-start.137 = (f32[128]{0:T(128)S(1)}, f32[128]{0:T(128)}, u32[]{:S(2)}) copy-start(f32[128]{0:T(128)} %copy-done.136) | copy-start | bytes 1540
  881.4 106.8 %copy-start.11 = (f32[128,1024]{1,0:T(8,128)S(1)}, f32[128,1024]{1,0:T(8,128)}, u32[]{:S(2)}) copy-start(f32[128,1024]{1,0:T(8,128)} %copy-done.10) | copy-start | bytes 1572868
  881.4 106.8 %copy-start.39 = (bf16[128,1024]{1,0:T(8,128)(2,1)S(1)}, bf16[128,1024]{1,0:T(8,128)(2,1)}, u32[]{:S(2)}) copy-start(bf16[128,1024]{1,0:T(8,128)(2,1)} %param.43) | copy-start | bytes 786436
  881.4 106.8 %copy-start.40 = (bf16[128,1024]{1,0:T(8,128)(2,1)S(1)}, bf16[128,1024]{1,0:T(8,128)(2,1)}, u32[]{:S(2)}) copy-start(bf16[128,1024]{1,0:T(8,128)(2,1)} %reduce-scatter.23.cloned.1.call-done) | copy-start | bytes 786436
  881.4 106.8 %copy-start.65 = (f32[1024]{0:T(1024)S(1)}, f32[1024]{0:T(1024)}, u32[]{:S(2)}) copy-start(f32[1024]{0:T(1024)} %param.39) | copy-start | bytes 12292
  881.4 106.8 %copy-start.118 = (f32[128]{0:T(128)S(1)}, f32[128]{0:T(128)}, u32[]{:S(2)}) copy-start(f32[128]{0:T(128)} %copy-done.117) | copy-start | bytes 1540
  881.5 106.8 %copy-start.135 = (f32[128]{0:T(128)S(1)}, f32[128]{0:T(128)}, u32[]{:S(2)}) copy-start(f32[128]{0:T(128)} %copy-done.134) | copy-start | bytes 1540
  (97 other events, 222.1 us)
Sparse Core Ops, SparseCore 0:
  11.5 30.6 all-gather.4
  302.2 43.0 reduce-scatter.18
  347.5 27.1 all-gather.6
  376.1 27.3 all-gather.8
  412.1 26.6 reduce-scatter.22
  443.8 26.4 all-gather.10
  846.6 33.5 reduce-scatter.42
  883.2 34.1 reduce-scatter.44
  919.7 27.2 reduce-scatter.24
  949.2 26.4 reduce-scatter.20
  979.7 43.2 reduce-scatter.36
  1026.8 44.6 reduce-scatter.38
  1075.5 44.6 reduce-scatter.40
  1123.9 35.9 reduce-scatter.28
  1163.5 35.9 reduce-scatter.26
  1203.2 41.1 reduce-scatter.34
  1248.0 41.1 reduce-scatter.30
  1292.9 41.1 reduce-scatter.32
where the time goes:
time: 1360 us; the launch traced here: 1340 us
  waiting for transfers between devices  545 us (40%)
  matrix products  308 us (23%)
  other arithmetic  273 us (20%)
  local copies, waits for them, and re-layouts  126 us (9%)
  blocking collectives  64.1 us (5%)
  between operations  16.4 us (1%)
    another operation x64, other arithmetic, delta_block(): lax.linalg.triangular_solve(system, right_side, left_side=True, lower=Tru...  165 us
    reduce_scatter x1, waiting for transfers between devices, body(): lax.psum_scatter(g_down, 'dp', scatter_dimension=1, tiled=True)  48.7 us
    reduce_scatter x1, waiting for transfers between devices, body(): lax.psum_scatter(g_fup, 'dp', scatter_dimension=0, tiled=True)  48.6 us
    reduce_scatter x1, waiting for transfers between devices, body(): lax.psum_scatter(g_out, 'dp', scatter_dimension=1, tiled=True)  44.9 us
    reduce_scatter x1, waiting for transfers between devices, body(): lax.psum_scatter(g_mats[3], 'dp', scatter_dimension=0, tiled=True)  44.9 us
    reduce_scatter x1, waiting for transfers between devices, body(): lax.psum_scatter(g_mats[2], 'dp', scatter_dimension=0, tiled=True)  44.9 us
    reduce_scatter x1, waiting for transfers between devices, body(): lax.psum_scatter(jnp.dot(rows_part, w_out, preferred_element_type=jnp.flo...  43.1 us
    psum x1, blocking collectives, body(): gain_parts = lax.psum((g_again, g_fgain, back[10]), ('dp', 'tensor'))  40 us
  transfers between devices with their start and end apart: 18, of which 16 were waited for; matrix products, arithmetic and copies ran while one was open for 4% of the time, Pallas kernels for 0%

commit v1 on v0

v1 whole, which is shorter than its diff:
```python
from functools import partial
import math

import jax
import jax.numpy as jnp
from jax import lax
from jax.experimental import pallas as pl
from jax.experimental.pallas import tpu as pltpu
from jax.sharding import PartitionSpec as P

GROUP = 64


EPS_NORM = 1e-05
EPS_UNIT = 1e-06
HIGH = lax.Precision.HIGHEST
MID = lax.Precision.HIGH


def norm_gain(values, gain):
    return values * lax.rsqrt(jnp.mean(values * values, axis=-1, keepdims=True) + EPS_NORM) * gain


def shift_rows(values, offset, fill):
    padding = jnp.full((offset,) + values.shape[1:], fill, values.dtype)
    return jnp.concatenate([padding, values[:-offset]], axis=0)


def short_conv(values, taps, seg_row):
    total = taps[0] * values
    for offset in range(1, taps.shape[0]):
        keep = (seg_row == shift_rows(seg_row, offset, -1)).astype(values.dtype)
        total = total + taps[offset] * shift_rows(values, offset, 0) * keep[:, None]
    return total


def unit_rows(values):
    return values * lax.rsqrt(jnp.sum(values * values, axis=-1, keepdims=True) + EPS_UNIT)


def inverse_kernel(lower_ref, out_ref):
    count, size, _ = lower_ref.shape
    rows = lax.broadcasted_iota(jnp.int32, (size, size), 0)
    cols = lax.broadcasted_iota(jnp.int32, (size, size), 1)
    lowers = [lower_ref[i] for i in range(count)]
    eye = (rows == cols).astype(jnp.float32)
    pair = (rows // 2 == cols // 2).astype(jnp.float32)
    done = [eye - low * pair for low in lowers]
    half = 2
    while half < size:
        keep = (rows // (2 * half) == cols // (2 * half)) & (rows // half != cols // half)
        keep = keep.astype(jnp.float32)
        steps = [
            jnp.dot(low * keep, inv, precision=HIGH, preferred_element_type=jnp.float32)
            for low, inv in zip(lowers, done)
        ]
        done = [
            inv - jnp.dot(inv, step, precision=HIGH, preferred_element_type=jnp.float32)
            for inv, step in zip(done, steps)
        ]
        half *= 2
    for i in range(count):
        out_ref[i] = done[i]


@jax.custom_vjp
def unit_inverse(lower):
    return inverse_of(lower)


def inverse_of(lower):
    count, size, _ = lower.shape
    return pl.pallas_call(
        inverse_kernel,
        out_shape=jax.ShapeDtypeStruct(lower.shape, jnp.float32),
        in_specs=[pl.BlockSpec(memory_space=pltpu.VMEM)],
        out_specs=pl.BlockSpec(memory_space=pltpu.VMEM),
        cost_estimate=pl.CostEstimate(
            flops=120 * count * size**3, bytes_accessed=8 * count * size**2, transcendentals=0
        ),
        name="unit_inverse",
    )(lower)


def inverse_forward(lower):
    inv = inverse_of(lower)
    return inv, inv


def inverse_backward(inv, d_inv):
    left = jnp.einsum("bji,bjk->bik", inv, d_inv, precision=HIGH)
    return (-jnp.einsum("bik,blk->bil", left, inv, precision=HIGH),)


unit_inverse.defvjp(inverse_forward, inverse_backward)


def mixer(
    seg_row,
    q_proj,
    k_proj,
    v_proj,
    gate_proj,
    decay_proj,
    beta_proj,
    conv_query,
    conv_key,
    conv_value,
    decay_rate,
    out_gain,
):
    length = q_proj.shape[0]
    heads = decay_proj.shape[1]
    key_dim = q_proj.shape[1] // heads
    val_dim = v_proj.shape[1] // heads
    blocks = length // GROUP
    pairs = heads * blocks

    def by_head(array, dim):
        parts = [array[:, h * dim : (h + 1) * dim] for h in range(heads)]
        return jnp.stack(parts).reshape(pairs, GROUP, dim)

    query = unit_rows(by_head(jax.nn.silu(short_conv(q_proj, conv_query, seg_row)), key_dim))
    query = query / math.sqrt(key_dim)
    keys = unit_rows(by_head(jax.nn.silu(short_conv(k_proj, conv_key, seg_row)), key_dim))
    values = by_head(jax.nn.silu(short_conv(v_proj, conv_value, seg_row)), val_dim)
    beta = jax.nn.sigmoid(beta_proj).T.reshape(pairs, GROUP)
    log_decay = (-decay_rate[None, :] * jax.nn.softplus(decay_proj)).T.reshape(pairs, GROUP)

    index = jnp.arange(GROUP)
    lower = index[:, None] >= index[None, :]
    strict = (index[:, None] > index[None, :]).astype(jnp.float32)
    doc = seg_row.reshape(blocks, GROUP)
    prev_doc = jnp.concatenate([jnp.full((1,), -1, doc.dtype), doc[:-1, -1]])
    same_doc = ((doc[:, :, None] == doc[:, None, :]) & lower[None]).astype(jnp.float32)
    same_doc = jnp.tile(same_doc, (heads, 1, 1))
    from_prev = jnp.tile((doc == prev_doc[:, None]).astype(jnp.float32), (heads, 1))

    cum_log = jnp.sum(log_decay[:, None, :] * lower.astype(jnp.float32)[None], axis=2)
    spread = jnp.exp(jnp.minimum(cum_log[:, :, None] - cum_log[:, None, :], 0.0)) * same_doc
    carried = jnp.exp(cum_log) * from_prev
    mm = partial(jnp.einsum, precision=MID)
    key_key = mm("btd,bid->bti", keys, keys)
    inverse = unit_inverse(beta[:, :, None] * key_key * spread * strict[None])
    fresh = mm("bti,bid->btd", inverse, beta[:, :, None] * values)
    erased = mm("bti,bid->btd", inverse, (beta * carried)[:, :, None] * keys)
    late_keys = keys * spread[:, -1, :, None]
    add = mm("bid,bie->bde", late_keys, fresh)
    move = carried[:, -1][:, None, None] * jnp.eye(key_dim, dtype=jnp.float32)[None]
    move = move - mm("bid,bie->bde", late_keys, erased)
    add = add.reshape(heads, blocks, key_dim, val_dim)
    move = move.reshape(heads, blocks, key_dim, key_dim)
    state = jnp.zeros((heads, key_dim, val_dim), jnp.float32)
    states = [state]
    for n in range(blocks - 1):
        if n == 0:
            state = add[:, 0]
        else:
            state = mm("hij,hje->hie", move[:, n], state) + add[:, n]
        states.append(state)
    entering = jnp.stack(states, axis=1).reshape(pairs, key_dim, val_dim)
    delta = fresh - mm("btd,bde->bte", erased, entering)
    query_key = mm("btd,bid->bti", query, keys) * spread
    mixed = mm("bti,bie->bte", query_key, delta)
    mixed = mixed + mm("btd,bde->bte", query * carried[:, :, None], entering)
    normed = mixed * lax.rsqrt(jnp.mean(mixed * mixed, axis=-1, keepdims=True) + EPS_NORM)
    normed = (normed * out_gain).reshape(heads, length, val_dim)
    normed = jnp.concatenate([normed[h] for h in range(heads)], axis=1)
    return normed * jax.nn.silu(gate_proj)


def body(
    tokens,
    seg_ids,
    attn_gain,
    w_query,
    w_key,
    w_value,
    w_gate,
    w_decay,
    w_beta,
    conv_query,
    conv_key,
    conv_value,
    decay_rate,
    out_gain,
    w_out,
    ffn_gain,
    w_ffn_gate,
    w_ffn_up,
    w_ffn_down,
    grad_out,
):
    seg_row = seg_ids[0]
    mats = (w_query, w_key, w_value, w_gate, w_decay, w_beta)
    x_float = tokens.astype(jnp.float32)
    xnorm_rows = norm_gain(x_float, attn_gain).astype(jnp.bfloat16)
    width = tokens.shape[1]
    both = lax.all_gather(
        jnp.concatenate([xnorm_rows, grad_out], axis=1), "tensor", axis=0, tiled=True
    )
    xnorm, grad_full = both[:, :width], both[:, width:]
    mats_cat = jnp.concatenate(mats, axis=1)
    cuts = []
    for weight in mats[:-1]:
        cuts.append(weight.shape[1] + (cuts[-1] if cuts else 0))
    projs = jnp.split(
        jnp.dot(xnorm, mats_cat, preferred_element_type=jnp.float32), cuts, axis=1
    )
    mixed, pull_mix = jax.vjp(
        partial(mixer, seg_row),
        projs[0],
        projs[1],
        projs[2],
        projs[3],
        projs[4],
        projs[5],
        conv_query,
        conv_key,
        conv_value,
        decay_rate,
        out_gain,
    )
    gated = mixed.astype(jnp.bfloat16)
    rows_part = gated
    resid = x_float + lax.psum_scatter(
        jnp.dot(rows_part, w_out, preferred_element_type=jnp.float32),
        "tensor",
        scatter_dimension=0,
        tiled=True,
    )
    hnorm_rows = norm_gain(resid, ffn_gain).astype(jnp.bfloat16)
    hnorm = lax.all_gather(hnorm_rows, "tensor", axis=0, tiled=True)
    up_in = jnp.dot(hnorm, w_ffn_gate, preferred_element_type=jnp.float32)
    up_val = jnp.dot(hnorm, w_ffn_up, preferred_element_type=jnp.float32)
    act = (jax.nn.silu(up_in) * up_val).astype(jnp.bfloat16)
    rows_part = act
    block_out = (
        resid
        + lax.psum_scatter(
            jnp.dot(rows_part, w_ffn_down, preferred_element_type=jnp.float32).astype(jnp.bfloat16),
            "tensor",
            scatter_dimension=0,
            tiled=True,
        ).astype(jnp.float32)
    ).astype(jnp.bfloat16)
    d_act = jnp.einsum("td,fd->tf", grad_full, w_ffn_down, preferred_element_type=jnp.float32)
    g_down = jnp.einsum("td,tf->df", grad_full, act, preferred_element_type=jnp.float32)
    gate_sig = jax.nn.sigmoid(up_in)
    d_up_in = (d_act * up_val * gate_sig * (1.0 + up_in * (1.0 - gate_sig))).astype(jnp.bfloat16)
    d_up_val = (d_act * up_in * gate_sig).astype(jnp.bfloat16)
    g_fgate = jnp.einsum("td,tf->df", hnorm, d_up_in, preferred_element_type=jnp.float32)
    g_fup = jnp.einsum("td,tf->df", hnorm, d_up_val, preferred_element_type=jnp.float32)
    total = jnp.einsum("tf,df->td", d_up_in, w_ffn_gate, preferred_element_type=jnp.float32)
    d_hnorm = lax.psum_scatter(
        (
            total + jnp.einsum("tf,df->td", d_up_val, w_ffn_up, preferred_element_type=jnp.float32)
        ).astype(jnp.bfloat16),
        "tensor",
        scatter_dimension=0,
        tiled=True,
    ).astype(jnp.float32)
    _, pull_mid = jax.vjp(norm_gain, resid, ffn_gain)
    d_resid_norm, g_fgain = pull_mid(d_hnorm)
    d_resid = grad_out.astype(jnp.float32) + d_resid_norm
    d_resid_full = lax.all_gather(d_resid.astype(jnp.bfloat16), "tensor", axis=0, tiled=True)
    g_out = jnp.einsum("td,tc->dc", d_resid_full, gated, preferred_element_type=jnp.float32)
    d_gated = jnp.einsum("td,cd->tc", d_resid_full, w_out, preferred_element_type=jnp.float32)
    back = pull_mix(d_gated)
    d_projs = [grad.astype(jnp.bfloat16) for grad in back[:6]]

    def sum_rows(parts):
        joined = jnp.concatenate([part.astype(jnp.bfloat16) for part in parts], axis=1)
        out = lax.psum_scatter(joined, "dp", scatter_dimension=0, tiled=True)
        edges = []
        for part in parts[:-1]:
            edges.append(part.shape[1] + (edges[-1] if edges else 0))
        return jnp.split(out.astype(jnp.float32), edges, axis=1)

    g_gate = jnp.einsum("td,tc->dc", xnorm, d_projs[3], preferred_element_type=jnp.float32)
    s_fgate, s_fup, s_down, s_out, s_gate = sum_rows((g_fgate, g_fup, g_down, g_out, g_gate))
    d_cat = jnp.concatenate(d_projs, axis=1)
    total = jnp.einsum("tc,dc->td", d_cat, mats_cat, preferred_element_type=jnp.float32)
    d_xnorm = lax.psum_scatter(
        total.astype(jnp.bfloat16), "tensor", scatter_dimension=0, tiled=True
    ).astype(jnp.float32)
    g_again = jnp.sum(total * (xnorm.astype(jnp.float32) / attn_gain), axis=0)
    _, pull_first = jax.vjp(lambda rows: norm_gain(rows, attn_gain), x_float)
    (d_x_norm,) = pull_first(d_xnorm)
    grad_tokens = (d_resid + d_x_norm).astype(jnp.bfloat16)
    rest = [d_projs[0], d_projs[1], d_projs[2], d_projs[4], d_projs[5]]
    g_rest = jnp.einsum(
        "td,tc->dc", xnorm, jnp.concatenate(rest, axis=1), preferred_element_type=jnp.float32
    ).astype(jnp.bfloat16)
    s_rest = lax.psum_scatter(g_rest, "dp", scatter_dimension=0, tiled=True).astype(jnp.float32)
    edges = []
    for part in rest[:-1]:
        edges.append(part.shape[1] + (edges[-1] if edges else 0))
    s_query, s_key, s_value, s_decay, s_beta = jnp.split(s_rest, edges, axis=1)
    weight_sums = (
        s_query, s_key, s_value, s_gate, s_decay, s_beta, s_out.T, s_fgate, s_fup, s_down.T
    )
    rate_parts = lax.psum((back[6], back[7], back[8], back[9]), "dp")
    gain_parts = lax.psum((g_again, g_fgain, back[10]), ("dp", "tensor"))
    return (
        block_out,
        grad_tokens,
        gain_parts[0],
        weight_sums[0],
        weight_sums[1],
        weight_sums[2],
        weight_sums[3],
        weight_sums[4],
        weight_sums[5],
        rate_parts[0],
        rate_parts[1],
        rate_parts[2],
        rate_parts[3],
        gain_parts[2],
        weight_sums[6],
        gain_parts[1],
        weight_sums[7],
        weight_sums[8],
        weight_sums[9],
    )


def solution(mesh):
    in_specs = (
        P(("dp", "tensor"), None),
        P("dp", None),
        P(),
        P(None, "tensor"),
        P(None, "tensor"),
        P(None, "tensor"),
        P(None, "tensor"),
        P(None, "tensor"),
        P(None, "tensor"),
        P(None, "tensor"),
        P(None, "tensor"),
        P(None, "tensor"),
        P("tensor"),
        P(),
        P("tensor", None),
        P(),
        P(None, "tensor"),
        P(None, "tensor"),
        P("tensor", None),
        P(("dp", "tensor"), None),
    )
    out_specs = (
        P(("dp", "tensor"), None),
        P(("dp", "tensor"), None),
        P(),
        P("dp", "tensor"),
        P("dp", "tensor"),
        P("dp", "tensor"),
        P("dp", "tensor"),
        P("dp", "tensor"),
        P("dp", "tensor"),
        P(None, "tensor"),
        P(None, "tensor"),
        P(None, "tensor"),
        P("tensor"),
        P(),
        P("tensor", "dp"),
        P(),
        P("dp", "tensor"),
        P("dp", "tensor"),
        P("tensor", "dp"),
    )
    return jax.shard_map(body, mesh=mesh, in_specs=in_specs, out_specs=out_specs, check_vma=False)
```

time: 1360 us -> 562 us (0.41)
  waiting for transfers between devices: 545 us -> 209 us
  matrix products: 308 us -> 93.7 us
  other arithmetic: 273 us -> 67 us
  local copies, waits for them, and re-layouts: 126 us -> 95.3 us
    reduce_scatter x8 -> x0, waiting for transfers between devices: 344 us -> none  [the longest x1 48.7 us: body(): lax.psum_scatter(g_down, 'dp', scatter_dimension=1, tiled=True)]
    dot_general x170 -> x53, matrix products: 244 us -> 70 us  [the longest x18 6.92 us: mixer(): state = mm('hij,hje->hie', move[:, n], state) + add[:, n]]
    another operation x106 -> x1, other arithmetic: 175 us -> 1.07 us  [by_head(): return jnp.stack(parts).reshape(pairs, GROUP, dim)]
    unnamed x20 -> x11, waiting for transfers between devices: 10.8 us -> 56.5 us
    dynamic_update_slice x48 -> x0, other arithmetic: 33.2 us -> none  [mixer(): lax.scan(delta_block, init, (split(query), split(keys), split(values), sp...]
    mul x50 -> x2, local copies, waits for them, and re-layouts: 32.1 us -> 0.75 us  [the longest x1 0.67 us: mixer(): log_decay[:, None, :] * lower.astype(jnp.float32)[None]]
    another operation x24 -> x0, matrix products: 30 us -> none  [delta_block(): lax.linalg.triangular_solve(system, right_side, left_side=True, lower=Tru...]
    reshape x16 -> x1, local copies, waits for them, and re-layouts: 28.3 us -> 0.08 us  [mixer(): (-decay_rate[None, :] * jax.nn.softplus(decay_proj)).T.reshape(pairs, GROUP)]
  transfers between devices with their start and end apart: 18 -> 9, of which waited for: 16 -> 6; matrix products, arithmetic and copies ran while one was open for 4% -> 11% of each run, Pallas kernels for 0% -> 0%
where the time goes in v1:
time: 562 us; the launch traced here: 554 us
  waiting for transfers between devices  209 us (37%)
  local copies, waits for them, and re-layouts  95.3 us (17%)
  matrix products  93.7 us (17%)
  other arithmetic  67 us (12%)
  blocking collectives  64.8 us (12%)
  between operations  16.6 us (3%)
  Pallas kernels  6.38 us (1%)
    unnamed x11, waiting for transfers between devices  56.5 us
    reduce_scatter x1, waiting for transfers between devices, body(): lax.psum_scatter(jnp.dot(rows_part, w_out, preferred_element_type=jnp.flo...  42.5 us
    psum x1, blocking collectives, body(): gain_parts = lax.psum((g_again, g_fgain, back[10]), ('dp', 'tensor'))  40.2 us
    unnamed x391, local copies, waits for them, and re-layouts  37.1 us
    all_gather x1, waiting for transfers between devices, body(): lax.all_gather(jnp.concatenate([xnorm_rows, grad_out], axis=1), 'tensor',...  30.2 us
    all_gather x1, waiting for transfers between devices, body(): hnorm = lax.all_gather(hnorm_rows, 'tensor', axis=0, tiled=True)  27.3 us
    reduce_scatter x1, waiting for transfers between devices, body(): lax.psum_scatter((total + jnp.einsum('tf,df->td', d_up_val, w_ffn_up, pre...  26.8 us
    all_gather x1, waiting for transfers between devices, body(): lax.all_gather(d_resid.astype(jnp.bfloat16), 'tensor', axis=0, tiled=True)  26.2 us
  transfers between devices with their start and end apart: 9, of which 6 were waited for; matrix products, arithmetic and copies ran while one was open for 11% of the time, Pallas kernels for 0%

profile of v1, /device:TPU:0, one launch (start us, length us, event | category | flops | bytes accessed | tf_op | source)
XLA Modules:
  0.0 554.0 jit_solution(6616729301618617274)
XLA Ops:
  9.7 1.8 pad_maximum_fusion.2
  14.8 6.1 %concatenate.70 = bf16[1024,1540]{1,0:T(8,128)(2,1)} concatenate(bf16[1024,256]{1,0:T(8,128)(2,1)S(1)} %copy-done.87, bf16[1024,256]{1,0:T(8,128)(2,1)} %param.24, bf16[1024,512]{1,0:T(8,128)(2,1)S(1)} %copy-done.79, bf16[1024,512]{1,0:T(8,128)(2,1)} %param.26, bf16[1024,2]{1,0:T(8,128)(2,1)S(1)} %copy.288, bf16[1024,2]{1,0:T(8,128)(2,1)S(1)} %copy.289), dimensions={1} | concatenate | bytes 6307840 | tf_op jit(solution)/shard_map/concatenate | solution.py:203
  27.5 1.5 fusion.147
  29.8 30.2 %all-gather.4.cloned.1.call-done = bf16[512,2048]{1,0:T(8,128)(2,1)} async-done(((bf16[128,2048]{1,0:T(8,128)(2,1)}), bf16[512,2048]{1,0:T(8,128)(2,1)}) %all-gather.4.cloned.1.call-update) | async-done | bytes 2097168 | tf_op jit(solution)/shard_map/all_gather | solution.py:199
  60.0 4.1 fusion.28
  74.3 3.7 fusion.55
  80.3 2.9 fusion.46
  83.2 6.4 %jvp_unit_inverse_.1 = f32[16,64,64]{2,1,0:T(8,128)} custom-call(f32[16,64,64]{2,1,0:T(8,128)} %get-tuple-element.228.lower_ref), custom_call_target="tpu_custom_call" | custom-call | flops 503316480 | bytes 524288 | tf_op jit(solution)/shard_map/jvp(unit_inverse)/pallas_call | solution.py:73
  91.1 4.4 fusion.16
  96.7 2.6 copy.293
  99.2 1.5 fusion.65
  113.3 2.0 copy.309
  116.3 1.9 multiply_convert_fusion.3
  118.3 2.1 fusion.150
  120.4 42.5 %reduce-scatter.11.cloned.1.call-done = f32[128,1024]{1,0:T(8,128)} async-done(((f32[512,1024]{1,0:T(8,128)}), f32[128,1024]{1,0:T(8,128)}) %reduce-scatter.11.cloned.1.call-update) | async-done | bytes 524304 | tf_op jit(solution)/shard_map/reduce_scatter | solution.py:226
  165.3 1.5 multiply_convert_fusion.4
  166.9 27.3 %all-gather.6.cloned.1.call-done = bf16[512,1024]{1,0:T(8,128)(2,1)} async-done(((bf16[128,1024]{1,0:T(8,128)(2,1)}), bf16[512,1024]{1,0:T(8,128)(2,1)}) %all-gather.6.cloned.1.call-update) | async-done | bytes 1048592 | tf_op jit(solution)/shard_map/all_gather | solution.py:233
  194.2 2.8 fusion.152
  198.5 2.4 multiply_convert_fusion
  202.8 2.0 add_convert_fusion
  204.9 26.8 %reduce-scatter.15.cloned.1.call-done = bf16[128,1024]{1,0:T(8,128)(2,1)} async-done(((bf16[512,1024]{1,0:T(8,128)(2,1)}), bf16[128,1024]{1,0:T(8,128)(2,1)}) %reduce-scatter.15.cloned.1.call-update) | async-done | bytes 262160 | tf_op jit(solution)/shard_map/reduce_scatter | solution.py:255
  231.7 1.7 fusion.33
  234.6 1.9 fusion.132
  237.0 26.2 %all-gather.8.cloned.1.call-done = bf16[512,1024]{1,0:T(8,128)(2,1)} async-done(((bf16[128,1024]{1,0:T(8,128)(2,1)}), bf16[512,1024]{1,0:T(8,128)(2,1)}) %all-gather.8.cloned.1.call-update) | async-done | bytes 1048592 | tf_op jit(solution)/shard_map/all_gather | solution.py:266
  263.2 4.0 fusion.14
  268.3 2.5 copy.312
  270.8 2.6 multiply_reduce_fusion.1
  274.7 1.5 fusion.155
  276.9 2.1 fusion.154
  290.1 2.0 fusion.157
  294.3 1.6 fusion.63
  298.6 1.6 pad_add_fusion
  302.8 2.1 convolution_add_fusion.4
  304.9 2.3 multiply_reduce_fusion.6
  307.3 1.5 convolution_add_fusion.7
  310.1 2.0 fusion.159
  312.2 2.2 fusion.43
  314.4 2.1 multiply_reduce_fusion.22
  318.8 2.3 multiply_reduce_fusion.21
  321.2 1.9 multiply_reduce_fusion.18
  333.4 3.2 multiply_reduce_fusion.13
  336.6 1.5 multiply_reduce_fusion.16
  345.5 2.1 copy.339
  347.5 2.1 copy.340
  349.6 3.2 multiply_reduce_fusion.5
  352.8 1.6 multiply_reduce_fusion.4
  359.0 1.7 multiply_reduce_fusion.10
  360.9 8.7 %concatenate.86 = bf16[512,1540]{0,1:T(8,128)(2,1)} concatenate(bf16[512,256]{0,1:T(8,128)(2,1)} %get-tuple-element.203, bf16[512,256]{0,1:T(8,128)(2,1)} %get-tuple-element.204, bf16[512,512]{0,1:T(8,128)(2,1)S(1)} %get-tuple-element.186, bf16[512,512]{0,1:T(8,128)(2,1)} %get-tuple-element.167, bf16[512,2]{0,1:T(2,128)(2,1)S(1)} %get-tuple-element.172, ...), dimensions={1} | concatenate | bytes 3153920 | tf_op jit(solution)/shard_map/concatenate | solution.py:282
  369.6 5.8 %multiply_reduce_fusion = (f32[1024]{0:T(1024)S(1)}, bf16[512,1024]{1,0:T(8,128)(2,1)}) fusion(f32[1024]{0:T(1024)S(1)} %copy-done.120, bf16[512,2048]{1,0:T(8,128)(2,1)} %all-gather.4.cloned.1.call-done, bf16[512,1540]{0,1:T(8,128)(2,1)} %concatenate.86, bf16[1024,1540]{1,0:T(8,128)(2,1)} %concatenate.70), kind=kOutput, calls=%fused_computation.1 | convolution fusion | flops 1617427456 | bytes 6836224 | tf_op jit(solution)/shard_map/tc,dc->td/dot_general | solution.py:283
  375.6 3.2 convolution_convert_fusion.4
  378.9 3.5 concatenate.87
  382.4 4.1 convolution_convert_fusion
  386.5 4.1 copy.364
  391.8 3.3 fusion.2
  395.1 2.1 fusion.1
  397.2 2.1 fusion
  399.2 1.8 fusion.4
  401.0 1.7 fusion.3
  402.7 9.5 %copy.366 = bf16[1024,3136]{1,0:T(8,128)(2,1)} copy(bf16[1024,3136]{0,1:T(8,128)(2,1)} %fusion.3) | data formatting | bytes 12845056
  412.9 40.2 %all-reduce.55 = (f32[1024]{0:T(1024)}, f32[256]{0:T(256)}, f32[1024]{0:T(1024)}) all-reduce(f32[1024]{0:T(1024)S(1)} %get-tuple-element.183, f32[256]{0:T(256)S(1)} %copy-done.153, f32[1024]{0:T(1024)S(1)} %copy-done.132), channel_id=1, replica_groups=mesh['dp'=8,'tensor'=4] {'dp','tensor'}, use_global_device_ids=true, to_apply=%region_25.26 | all-reduce | flops 2304 | bytes 18432 | tf_op jit(solution)/shard_map/psum | solution.py:304
  453.3 24.6 %all-reduce.56 = (f32[4,256]{1,0:T(4,128)}, f32[4,256]{1,0:T(4,128)}, f32[4,512]{1,0:T(4,128)}, f32[2]{0:T(128)}) all-reduce(f32[4,256]{1,0:T(4,128)S(1)} %pad_add_fusion.5, f32[4,256]{1,0:T(4,128)S(1)} %pad_add_fusion.4, f32[4,512]{1,0:T(4,128)S(1)} %pad_add_fusion.3, f32[2]{0:T(128)S(1)} %neg.64), channel_id=1, replica_groups=mesh['dp'=8,'tensor'=4] {'dp'}, use_global_device_ids=true, to_apply=%region_32.33 | all-reduce | flops 4098 | bytes 32784 | tf_op jit(solution)/shard_map/psum | solution.py:303
  479.1 2.1 fusion.40
  485.3 56.3 %reduce-scatter.21.cloned.1.call-done = bf16[128,3136]{1,0:T(8,128)(2,1)} async-done(((bf16[1024,3136]{1,0:T(8,128)(2,1)}), bf16[128,3136]{1,0:T(8,128)(2,1)}) %reduce-scatter.21.cloned.1.call-update) | async-done | bytes 802832
  541.7 2.0 copy.367
  (552 shorter events, 106.5 us)
Async XLA Ops:
  7.2 190.7 %copy-start = (bf16[704,1024]{1,0:T(8,128)(2,1)S(1)}, bf16[704,1024]{1,0:T(8,128)(2,1)}, u32[]{:S(2)}) copy-start(bf16[704,1024]{1,0:T(8,128)(2,1)} %param.38) | copy-start | bytes 4325380
  7.2 4.4 copy-start.183
  7.2 5.5 copy-start.119
  7.2 7.1 %copy-start.154 = (bf16[1024,2]{0,1:T(2,128)(2,1)S(1)}, bf16[1024,2]{0,1:T(2,128)(2,1)}, u32[]{:S(2)}) copy-start(bf16[1024,2]{0,1:T(2,128)(2,1)} %param.27) | copy-start | bytes 12292
  7.2 7.3 %copy-start.155 = (bf16[1024,2]{0,1:T(2,128)(2,1)S(1)}, bf16[1024,2]{0,1:T(2,128)(2,1)}, u32[]{:S(2)}) copy-start(bf16[1024,2]{0,1:T(2,128)(2,1)} %param.28) | copy-start | bytes 12292
  7.2 7.5 %copy-start.79 = (bf16[1024,512]{1,0:T(8,128)(2,1)S(1)}, bf16[1024,512]{1,0:T(8,128)(2,1)}, u32[]{:S(2)}) copy-start(bf16[1024,512]{1,0:T(8,128)(2,1)} %param.25) | copy-start | bytes 3145732
  7.3 7.5 %copy-start.87 = (bf16[1024,256]{1,0:T(8,128)(2,1)S(1)}, bf16[1024,256]{1,0:T(8,128)(2,1)}, u32[]{:S(2)}) copy-start(bf16[1024,256]{1,0:T(8,128)(2,1)} %param.23) | copy-start | bytes 1572868
  7.3 52.8 %all-gather.4.cloned.1.call-start = ((), (), s32[]{:S(2)}) async-start(), calls=%async_computation.6 | async-start | bytes 2621440 | tf_op jit(solution)/shard_map/all_gather | solution.py:199
  8.5 5.8 %copy-start.173 = (f32[128]{0:T(128)}, f32[128]{0:T(128)S(1)}, u32[]{:S(2)}) copy-start(f32[128]{0:T(128)S(1)} %fusion.48) | copy-start | bytes 1540
  8.6 5.0 copy-start.169
  11.5 151.4 %reduce-scatter.11.cloned.1.call-start = ((), (), s32[]{:S(2)}) async-start(), calls=%async_computation.7 | async-start | bytes 2621440 | tf_op jit(solution)/shard_map/reduce_scatter | solution.py:226
  14.8 8.7 %copy-start.164 = (f32[4,256]{1,0:T(4,128)S(1)}, f32[4,256]{1,0:T(4,128)}, u32[]{:S(2)}) copy-start(f32[4,256]{1,0:T(4,128)} %param.29) | copy-start | bytes 12292
  64.2 4.6 copy-start.3
  68.7 9.4 %copy-start.30 = (f32[510,256]{0,1:T(8,128)}, f32[510,256]{0,1:T(8,128)S(1)}, u32[]{:S(2)}) copy-start(f32[510,256]{0,1:T(8,128)S(1)} %get-tuple-element.175) | copy-start | bytes 1566724
  68.7 9.4 %copy-start.32 = (f32[510,256]{0,1:T(8,128)}, f32[510,256]{0,1:T(8,128)S(1)}, u32[]{:S(2)}) copy-start(f32[510,256]{0,1:T(8,128)S(1)} %get-tuple-element.176) | copy-start | bytes 1566724
  69.3 8.8 %copy-start.34 = (f32[511,256]{0,1:T(8,128)}, f32[511,256]{0,1:T(8,128)S(1)}, u32[]{:S(2)}) copy-start(f32[511,256]{0,1:T(8,128)S(1)} %get-tuple-element.173) | copy-start | bytes 1569796
  69.3 8.8 %copy-start.36 = (f32[511,256]{0,1:T(8,128)}, f32[511,256]{0,1:T(8,128)S(1)}, u32[]{:S(2)}) copy-start(f32[511,256]{0,1:T(8,128)S(1)} %get-tuple-element.174) | copy-start | bytes 1569796
  70.7 7.4 %copy-start.81 = (f32[16,64]{1,0:T(8,128)}, f32[16,64]{1,0:T(8,128)S(1)}, u32[]{:S(2)}) copy-start(f32[16,64]{1,0:T(8,128)S(1)} %mul.997) | copy-start | bytes 12292
  79.3 3.9 copy-start.89
  80.3 9.4 %copy-start.38 = (f32[16,64,64]{2,1,0:T(8,128)}, f32[16,64,64]{2,1,0:T(8,128)S(1)}, u32[]{:S(2)}) copy-start(f32[16,64,64]{2,1,0:T(8,128)S(1)} %fusion.106) | copy-start | bytes 786436
  80.3 10.8 %copy-start.113 = (f32[512]{0:T(512)S(1)}, f32[512]{0:T(512)}, u32[]{:S(2)}) copy-start(f32[512]{0:T(512)} %get-tuple-element.257) | copy-start | bytes 6148
  80.3 10.8 %copy-start.115 = (f32[512]{0:T(512)S(1)}, f32[512]{0:T(512)}, u32[]{:S(2)}) copy-start(f32[512]{0:T(512)} %get-tuple-element.258) | copy-start | bytes 6148
  80.3 10.8 %copy-start.117 = (f32[512]{0:T(512)S(1)}, f32[512]{0:T(512)}, u32[]{:S(2)}) copy-start(f32[512]{0:T(512)} %get-tuple-element.256) | copy-start | bytes 6148
  80.3 10.8 %copy-start.124 = (f32[1,512]{1,0:T(1,128)S(1)}, f32[1,512]{1,0:T(1,128)}, u32[]{:S(2)}) copy-start(f32[1,512]{1,0:T(1,128)} %get-tuple-element.239) | copy-start | bytes 6148
  80.3 10.8 %copy-start.126 = (f32[1,512]{1,0:T(1,128)S(1)}, f32[1,512]{1,0:T(1,128)}, u32[]{:S(2)}) copy-start(f32[1,512]{1,0:T(1,128)} %get-tuple-element.241) | copy-start | bytes 6148
  80.3 10.8 %copy-start.128 = (f32[1,512]{1,0:T(1,128)S(1)}, f32[1,512]{1,0:T(1,128)}, u32[]{:S(2)}) copy-start(f32[1,512]{1,0:T(1,128)} %get-tuple-element.240) | copy-start | bytes 6148
  80.3 10.8 %copy-start.130 = (f32[1,512]{1,0:T(1,128)S(1)}, f32[1,512]{1,0:T(1,128)}, u32[]{:S(2)}) copy-start(f32[1,512]{1,0:T(1,128)} %get-tuple-element.242) | copy-start | bytes 6148
  95.6 3.6 copy-start.5
  100.7 7.5 %copy-start.14 = (f32[16,64,128]{2,1,0:T(8,128)}, f32[16,64,128]{2,1,0:T(8,128)S(1)}, u32[]{:S(2)}) copy-start(f32[16,64,128]{2,1,0:T(8,128)S(1)} %fusion.65) | copy-start | bytes 1572868
  102.1 6.1 %copy-start.10 = (f32[16,64,256]{2,1,0:T(8,128)}, f32[16,64,256]{2,1,0:T(8,128)S(1)}, u32[]{:S(2)}) copy-start(f32[16,64,256]{2,1,0:T(8,128)S(1)} %fusion.21) | copy-start | bytes 3145732
  120.4 73.8 %all-gather.6.cloned.1.call-start = ((), (), s32[]{:S(2)}) async-start(), calls=%async_computation.8 | async-start | bytes 1310720 | tf_op jit(solution)/shard_map/all_gather | solution.py:233
  166.8 64.8 %reduce-scatter.15.cloned.1.call-start = ((), (), s32[]{:S(2)}) async-start(), calls=%async_computation.10 | async-start | bytes 1310720 | tf_op jit(solution)/shard_map/reduce_scatter | solution.py:255
  204.8 58.4 %all-gather.8.cloned.1.call-start = ((), (), s32[]{:S(2)}) async-start(), calls=%async_computation.11 | async-start | bytes 1310720 | tf_op jit(solution)/shard_map/all_gather | solution.py:266
  236.6 241.3 %reduce-scatter.17.cloned.1.call-start = ((), (), s32[]{:S(2)}) async-start(), calls=%async_computation.12 | async-start | bytes 1310720 | tf_op jit(solution)/shard_map/reduce_scatter | solution.py:284
  276.8 4.8 copy-start.12
  284.8 3.7 copy-start.44
  285.1 4.1 copy-start.86
  321.2 4.0 copy-start.73
  338.1 4.2 copy-start.143
  339.2 4.2 copy-start.142
  340.2 4.2 copy-start.42
  344.4 5.2 copy-start.118
  360.8 8.9 %copy-start.120 = (f32[1024]{0:T(1024)S(1)}, f32[1024]{0:T(1024)}, u32[]{:S(2)}) copy-start(f32[1024]{0:T(1024)} %param.22) | copy-start | bytes 12292
  375.5 103.6 %reduce-scatter.13.cloned.1.call-start = ((), (), s32[]{:S(2)}) async-start(), calls=%async_computation.9 | async-start | bytes 1310720 | tf_op jit(solution)/shard_map/reduce_scatter | solution.py:240
  378.8 102.4 %reduce-scatter.19.cloned.1.call-start = ((), (), s32[]{:S(2)}) async-start(), calls=%async_computation.13 | async-start | bytes 2654208
  390.6 151.1 %reduce-scatter.21.cloned.1.call-start = ((), (), s32[]{:S(2)}) async-start(), calls=%async_computation.14 | async-start | bytes 7372800
  412.3 40.9 %copy-start.157 = (f32[256]{0:T(256)S(1)}, f32[256]{0:T(256)}, u32[]{:S(2)}) copy-start(f32[256]{0:T(256)} %get-tuple-element.141) | copy-start | bytes 3076
  412.3 40.9 %copy-start.160 = (f32[256]{0:T(256)S(1)}, f32[256]{0:T(256)}, u32[]{:S(2)}) copy-start(f32[256]{0:T(256)} %get-tuple-element.243) | copy-start | bytes 3076
  412.3 40.9 %copy-start.161 = (f32[256]{0:T(256)S(1)}, f32[256]{0:T(256)}, u32[]{:S(2)}) copy-start(f32[256]{0:T(256)} %get-tuple-element.245) | copy-start | bytes 3076
  412.3 40.9 %copy-start.163 = (f32[256]{0:T(256)S(1)}, f32[256]{0:T(256)}, u32[]{:S(2)}) copy-start(f32[256]{0:T(256)} %get-tuple-element.114) | copy-start | bytes 3076
  412.3 40.9 %copy-start.156 = (f32[256]{0:T(256)S(1)}, f32[256]{0:T(256)}, u32[]{:S(2)}) copy-start(f32[256]{0:T(256)} %get-tuple-element.259) | copy-start | bytes 3076
  412.3 40.9 %copy-start.158 = (f32[256]{0:T(256)S(1)}, f32[256]{0:T(256)}, u32[]{:S(2)}) copy-start(f32[256]{0:T(256)} %get-tuple-element.151) | copy-start | bytes 3076
  412.3 40.9 %copy-start.159 = (f32[256]{0:T(256)S(1)}, f32[256]{0:T(256)}, u32[]{:S(2)}) copy-start(f32[256]{0:T(256)} %get-tuple-element.213) | copy-start | bytes 3076
  412.3 40.9 %copy-start.162 = (f32[256]{0:T(256)S(1)}, f32[256]{0:T(256)}, u32[]{:S(2)}) copy-start(f32[256]{0:T(256)} %get-tuple-element.115) | copy-start | bytes 3076
  412.3 40.9 %copy-start.148 = (f32[512]{0:T(512)S(1)}, f32[512]{0:T(512)}, u32[]{:S(2)}) copy-start(f32[512]{0:T(512)} %get-tuple-element.189) | copy-start | bytes 6148
  412.4 40.9 %copy-start.149 = (f32[512]{0:T(512)S(1)}, f32[512]{0:T(512)}, u32[]{:S(2)}) copy-start(f32[512]{0:T(512)} %get-tuple-element.134) | copy-start | bytes 6148
  412.4 65.5 %copy-start.24 = (bf16[128,1024]{1,0:T(8,128)(2,1)S(1)}, bf16[128,1024]{1,0:T(8,128)(2,1)}, u32[]{:S(2)}) copy-start(bf16[128,1024]{1,0:T(8,128)(2,1)} %param.20) | copy-start | bytes 786436
  412.4 66.7 %copy-start.174 = (f32[128]{0:T(128)S(1)}, f32[128]{0:T(128)}, u32[]{:S(2)}) copy-start(f32[128]{0:T(128)} %copy-done.173) | copy-start | bytes 1540
  412.4 66.7 %copy-start.63 = (bf16[128,1024]{1,0:T(8,128)(2,1)S(1)}, bf16[128,1024]{1,0:T(8,128)(2,1)}, u32[]{:S(2)}) copy-start(bf16[128,1024]{1,0:T(8,128)(2,1)} %reduce-scatter.15.cloned.1.call-done) | copy-start | bytes 786436
  412.4 66.7 %copy-start.64 = (bf16[128,1024]{1,0:T(8,128)(2,1)S(1)}, bf16[128,1024]{1,0:T(8,128)(2,1)}, u32[]{:S(2)}) copy-start(bf16[128,1024]{1,0:T(8,128)(2,1)} %param.39) | copy-start | bytes 786436
  412.4 66.7 %copy-start.112 = (f32[1024]{0:T(1024)S(1)}, f32[1024]{0:T(1024)}, u32[]{:S(2)}) copy-start(f32[1024]{0:T(1024)} %param.35) | copy-start | bytes 12292
  412.4 66.7 %copy-start.152 = (f32[128]{0:T(128)S(1)}, f32[128]{0:T(128)}, u32[]{:S(2)}) copy-start(f32[128]{0:T(128)} %copy-done.151) | copy-start | bytes 1540
  412.4 66.7 %copy-start.170 = (f32[128]{0:T(128)S(1)}, f32[128]{0:T(128)}, u32[]{:S(2)}) copy-start(f32[128]{0:T(128)} %copy-done.169) | copy-start | bytes 1540
  412.4 66.7 %copy-start.172 = (f32[128]{0:T(128)S(1)}, f32[128]{0:T(128)}, u32[]{:S(2)}) copy-start(f32[128]{0:T(128)} %copy-done.171) | copy-start | bytes 1540
  (133 other events, 259.3 us)
Sparse Core Ops, SparseCore 0:
  11.6 48.3 all-gather.3
  120.5 42.4 reduce-scatter.10
  166.9 27.1 all-gather.5
  204.9 26.6 reduce-scatter.14
  236.7 26.4 all-gather.7
  375.6 26.6 reduce-scatter.16
  404.6 25.7 reduce-scatter.12
  433.8 41.4 reduce-scatter.18
  478.7 62.9 reduce-scatter.20
